TPU v7x, 256 devices: a whole 4x4x8 slice. The times are simulated.
256 devices in a mesh: past: 32 (over y, x, core), second: 8 (over z).
Axes of the slice: x: 4, y: 4, z: 8, core: 2. Of those that a mesh axis runs over, the one named last changes fastest.
Arguments:
- g_hist: bfloat16 [65536, 8192], P('past', 'second'), may hold values from -6 to 6
- sigma_hist: bfloat16 [1024, 65536], P(None, 'past'), may hold values from -0.046875 to 0.046875
- volterra: bfloat16 [2, 512, 1024], replicated, may hold values from -0.1875 to 0.1875
- sigma_edge: bfloat16 [512, 8192], P(None, 'second'), may hold values from -6 to 6
- coupling: float32 [32, 8192], P(None, 'second'), may hold values from 0.3 to 3
Outputs:
- g_new: bfloat16 [1024, 8192], P(None, 'second')
- sigma_new: bfloat16 [1024, 8192], P(None, 'second')
All inputs are finite; a program needn't handle non-finite values.
Results may differ from a plain program's by a relative error of at most 0.0059.
Values may be sent and summed in bfloat16 or wider, within the bound.
A program may use at most 64 MiB of HBM per device.

v0:
```python
import jax
import jax.numpy as jnp
from jax import lax
from jax.sharding import PartitionSpec as P

N = 32
BLK = 16
NB = 2


def per_device(g_hist, sigma_hist, volterra, sigma_edge, coupling):
    rows = BLK * N
    columns = g_hist.shape[1]
    count_all = rows * columns * lax.axis_size("second")
    prev = sigma_edge
    g_blocks = []
    s_blocks = []
    for block in range(NB):
        sig_rows = sigma_hist[block * rows : (block + 1) * rows, :]
        w_memory = volterra[block][:, :rows]
        w_sigma = volterra[block][:, rows:]
        start_value = jnp.dot(w_sigma, prev, preferred_element_type=jnp.float32)
        mine = lax.psum_scatter(
            jnp.dot(sig_rows, g_hist, preferred_element_type=jnp.float32),
            "past",
            scatter_dimension=0,
            tiled=True,
        ).astype(jnp.bfloat16)
        gnew = start_value + jnp.dot(
            w_memory,
            lax.all_gather(mine, "past", axis=0, tiled=True),
            preferred_element_type=jnp.float32,
        )
        cubic = gnew.reshape(BLK, N, columns) ** 3 * coupling[None]
        local_sq = jnp.sum(cubic * cubic)
        total_sq = lax.psum(local_sq, "second")
        meansq = total_sq / count_all
        sigma = (cubic / jnp.sqrt(meansq + 1e-06)).reshape(rows, columns).astype(jnp.bfloat16)
        g_blocks.append(gnew.astype(jnp.bfloat16))
        s_blocks.append(sigma)
        prev = sigma
    return (jnp.concatenate(g_blocks, axis=0), jnp.concatenate(s_blocks, axis=0))


def solution(mesh):
    return jax.shard_map(
        per_device,
        mesh=mesh,
        in_specs=(P("past", "second"), P(None, "past"), P(), P(None, "second"), P(None, "second")),
        out_specs=(P(None, "second"), P(None, "second")),
        check_vma=False,
    )
```

profile of v0, /device:TPU:1, one launch (start us, length us, event | category | flops | bytes accessed | tf_op | source)
XLA Modules:
  0.0 326.4 jit_solution(678575552743775766)
XLA Ops:
  7.2 0.0 copy-start
  7.2 0.0 reduce-scatter.3.cloned.1.call-start
  7.2 6.5 %fusion.2 = f32[512,1024]{1,0:T(8,128)} fusion(bf16[2048,1024]{1,0:T(8,128)(2,1)} %param.5, bf16[1024,2048]{1,0:T(8,128)(2,1)} %param.6), kind=kOutput, calls=%fused_computation.14 | convolution fusion | flops 2147483648 | bytes 8388608 | tf_op jit(solution)/shard_map/dot_general | solution.py:24
  13.8 0.0 reduce-scatter.3.cloned.1.call-update
  13.8 0.0 reduce-scatter.5.cloned.1.call-start
  13.8 6.5 %fusion = f32[512,1024]{1,0:T(8,128)} fusion(bf16[2048,1024]{1,0:T(8,128)(2,1)} %param.5, bf16[1024,2048]{1,0:T(8,128)(2,1)} %param.6), kind=kOutput, calls=%fused_computation.10 | convolution fusion | flops 2147483648 | bytes 8388608 | tf_op jit(solution)/shard_map/dot_general | solution.py:24
  20.3 0.0 copy-start.8
  20.3 0.0 reduce-scatter.5.cloned.1.call-update
  20.3 0.0 all-gather.3.cloned.1.call-start
  20.4 82.2 %reduce-scatter.3.cloned.1.call-done = f32[16,1024]{1,0:T(8,128)} async-done(((f32[512,1024]{1,0:T(8,128)}), f32[16,1024]{1,0:T(8,128)}) %reduce-scatter.3.cloned.1.call-update) | async-done | bytes 65552 | tf_op jit(solution)/shard_map/reduce_scatter | solution.py:23
  102.6 1.5 convert_element_type.18
  104.1 0.0 all-gather.3.cloned.1.call-update
  104.1 0.0 all-gather.5.cloned.1.call-start
  104.2 88.9 %reduce-scatter.5.cloned.1.call-done = f32[16,1024]{1,0:T(8,128)} async-done(((f32[512,1024]{1,0:T(8,128)}), f32[16,1024]{1,0:T(8,128)}) %reduce-scatter.5.cloned.1.call-update) | async-done | bytes 65552 | tf_op jit(solution)/shard_map/reduce_scatter | solution.py:23
  193.0 1.4 convert_element_type.21
  194.5 0.0 all-gather.5.cloned.1.call-update
  194.5 0.0 copy-done.8
  194.5 1.1 slice_bitcast_fusion
  195.6 0.0 copy-start.4
  195.6 0.0 copy-start.7
  195.6 1.0 copy-done.4
  196.6 0.0 copy-done
  196.6 0.7 fusion.8
  197.3 47.9 %all-gather.3.cloned.1.call-done = bf16[512,1024]{1,0:T(8,128)(2,1)} async-done(((bf16[16,1024]{1,0:T(8,128)(2,1)}), bf16[512,1024]{1,0:T(8,128)(2,1)}) %all-gather.3.cloned.1.call-update) | async-done | bytes 1048592 | tf_op jit(solution)/shard_map/all_gather | solution.py:31
  245.2 0.0 copy-done.7
  245.2 4.1 %multiply_reduce_fusion.1 = (f32[]{:T(128)}, f32[512,1024]{1,0:T(8,128)}) fusion(f32[32,1024]{1,0:T(8,128)S(1)} %copy-done.7, f32[512,1024]{1,0:T(8,128)S(1)} %fusion.8, bf16[512,1024]{1,0:T(8,128)(2,1)} %all-gather.3.cloned.1.call-done, bf16[512,1024]{1,0:T(8,128)(2,1)} %copy-done.4), kind=kOutput, calls=%fused_computation.13 | convolution fusion | flops 540016640 | bytes 5898244 | tf_op jit(solution)/shard_map/dot_general | solution.py:29
  249.3 14.5 %psum.14 = f32[]{:T(128)} all-reduce(f32[]{:T(128)} %get-tuple-element.6), channel_id=1, replica_groups=mesh['past'=32,'second'=8] {'second'}, use_global_device_ids=true, to_apply=%region_2.0 | all-reduce | flops 1 | bytes 8 | tf_op jit(solution)/shard_map/psum | solution.py:36
  264.6 0.0 copy-start.5
  264.6 3.8 %fusion.10 = (bf16[512,1024]{1,0:T(8,128)(2,1)}, bf16[512,1024]{1,0:T(8,128)(2,1)S(1)}) fusion(f32[512,1024]{1,0:T(8,128)} %get-tuple-element.7, f32[]{:T(128)S(6)} %sqrt.6, f32[32,1024]{1,0:T(8,128)S(1)} %copy-done.7), kind=kLoop, calls=%fused_computation.25 | loop fusion | flops 3145728 | bytes 4325380 | tf_op jit(solution)/shard_map/convert_element_type | solution.py:39
  268.4 0.0 copy-start.1
  268.4 1.0 copy-done.1
  269.4 0.0 copy-done.5
  269.4 2.0 fusion.5
  271.4 23.3 %all-gather.5.cloned.1.call-done = bf16[512,1024]{1,0:T(8,128)(2,1)} async-done(((bf16[16,1024]{1,0:T(8,128)(2,1)}), bf16[512,1024]{1,0:T(8,128)(2,1)}) %all-gather.5.cloned.1.call-update) | async-done | bytes 1048592 | tf_op jit(solution)/shard_map/all_gather | solution.py:31
  294.7 3.8 %bitcast_convert_fusion = (bf16[512,1024]{1,0:T(8,128)(2,1)}, f32[1024,512]{0,1:T(8,128)S(1)}) fusion(f32[1024,512]{0,1:T(8,128)} %fusion.5, bf16[512,1024]{1,0:T(8,128)(2,1)} %all-gather.5.cloned.1.call-done, bf16[512,1024]{1,0:T(8,128)(2,1)} %get-tuple-element.4), kind=kOutput, calls=%fused_computation.6 | convolution fusion | flops 537919488 | bytes 6815744 | tf_op jit(solution)/shard_map/dot_general | solution.py:29
  298.4 1.1 multiply_reduce_fusion
  299.6 14.5 %psum.15 = f32[]{:T(128)} all-reduce(f32[]{:T(128)} %multiply_reduce_fusion), channel_id=1, replica_groups=mesh['past'=32,'second'=8] {'second'}, use_global_device_ids=true, to_apply=%region_5.0 | all-reduce | flops 1 | bytes 8 | tf_op jit(solution)/shard_map/psum | solution.py:36
  314.8 0.0 copy-start.2
  314.8 0.3 divide_convert_fusion
  315.2 0.9 copy-done.2
  316.0 0.0 copy-start.3
  316.0 0.0 copy-start.6
  316.0 1.5 pad_maximum_fusion.1
  317.5 0.0 copy-done.3
  317.6 0.8 copy-done.6
  318.3 1.5 pad_maximum_fusion
Async XLA Ops:
  7.2 189.5 %copy-start = (bf16[512,1024]{1,0:T(8,128)(2,1)S(1)}, bf16[512,1024]{1,0:T(8,128)(2,1)}, u32[]{:S(2)}) copy-start(bf16[512,1024]{1,0:T(8,128)(2,1)} %param.8) | copy-start | bytes 3145732
  7.2 95.4 %reduce-scatter.3.cloned.1.call-start = ((), (), s32[]{:S(2)}) async-start(), calls=%async_computation.2 | async-start | bytes 2162688 | tf_op jit(solution)/shard_map/reduce_scatter | solution.py:23
  13.8 179.2 %reduce-scatter.5.cloned.1.call-start = ((), (), s32[]{:S(2)}) async-start(), calls=%async_computation.4 | async-start | bytes 2162688 | tf_op jit(solution)/shard_map/reduce_scatter | solution.py:23
  20.3 174.2 %copy-start.8 = (bf16[2,512,1024]{2,1,0:T(8,128)(2,1)S(1)}, bf16[2,512,1024]{2,1,0:T(8,128)(2,1)}, u32[]{:S(2)}) copy-start(bf16[2,512,1024]{2,1,0:T(8,128)(2,1)} %param.7) | copy-start | bytes 6291460
  20.3 224.9 %all-gather.3.cloned.1.call-start = ((), (), s32[]{:S(2)}) async-start(), calls=%async_computation.3 | async-start | bytes 1081344 | tf_op jit(solution)/shard_map/all_gather | solution.py:31
  104.1 190.6 %all-gather.5.cloned.1.call-start = ((), (), s32[]{:S(2)}) async-start(), calls=%async_computation.5 | async-start | bytes 1081344 | tf_op jit(solution)/shard_map/all_gather | solution.py:31
  195.6 1.0 copy-start.4
  195.6 49.6 %copy-start.7 = (f32[32,1024]{1,0:T(8,128)S(1)}, f32[32,1024]{1,0:T(8,128)}, u32[]{:S(2)}) copy-start(f32[32,1024]{1,0:T(8,128)} %param.9) | copy-start | bytes 393220
  264.6 4.8 %copy-start.5 = (bf16[512,1024]{1,0:T(8,128)(2,1)S(1)}, bf16[512,1024]{1,0:T(8,128)(2,1)}, u32[]{:S(2)}) copy-start(bf16[512,1024]{1,0:T(8,128)(2,1)} %get-tuple-element.4) | copy-start | bytes 3145732
  268.4 1.0 copy-start.1
  314.8 1.2 copy-start.2
  316.0 1.5 copy-start.3
  316.0 2.3 copy-start.6
Sparse Core Ops, SparseCore 0:
  13.9 88.6 reduce-scatter.2
  107.0 85.9 reduce-scatter.4
  196.1 49.0 all-gather.2
  247.7 46.9 all-gather.4
where the time goes:
time: 329 us; the launch traced here: 326 us
  waiting for transfers between devices  242 us (74%)
  blocking collectives  29.1 us (9%)
  matrix products  23.6 us (7%)
  between operations  15.2 us (5%)
  other arithmetic  11.2 us (3%)
  local copies, waits for them, and re-layouts  4.8 us (1%)
    reduce_scatter x2, waiting for transfers between devices, per_device(): lax.psum_scatter(jnp.dot(sig_rows, g_hist, preferred_element_type=jnp.flo...  171 us
    all_gather x2, waiting for transfers between devices, per_device(): lax.all_gather(mine, 'past', axis=0, tiled=True)  71.2 us
    psum x2, blocking collectives, per_device(): total_sq = lax.psum(local_sq, 'second')  29.1 us
    dot_general x2, matrix products, per_device(): jnp.dot(sig_rows, g_hist, preferred_element_type=jnp.float32)  13 us
    dot_general x2, matrix products, per_device(): jnp.dot(w_memory, lax.all_gather(mine, 'past', axis=0, tiled=True), prefe...  7.87 us
  transfers between devices with their start and end apart: 4, of which 4 were waited for; matrix products, arithmetic and copies ran while one was open for 6% of the time, Pallas kernels for 0%

commit v1 on v0

v1 whole, which is shorter than its diff:
```python
import functools

import jax
import jax.numpy as jnp
from jax import lax
from jax.experimental import pallas as pl
from jax.experimental.pallas import tpu as pltpu
from jax.sharding import PartitionSpec as P

N = 32
MESH = pl.DeviceIdType.MESH
F32 = jnp.float32
BF16 = jnp.bfloat16
RING = 4
CHUNKS = 4


def dot(a, b):
    return jnp.dot(a, b, preferred_element_type=F32)


def kernel(
    n_z, count_all,
    g_hbm, sig_hbm, vol_hbm, edge_hbm, coup_hbm, g_out, s_out,
    g, sig, vol, edge, coup, psend, precv, own, a_buf, ra, a2, rb, b_buf, b_f32, rc, mem, s_buf, cubic, stat,
    send_sem, recv_sem, load_sem,
):
    rows = mem.shape[1]
    half = rows // 2
    sub = half // RING
    hs = sub // 2
    piece = sub // RING
    width = mem.shape[2]
    tile = min(256, width)

    past = lax.axis_index("past")
    z = lax.axis_index("second")
    core = lax.rem(past, 2)
    x = lax.rem(past // 2, RING)
    y = past // (2 * RING)
    s = x * (1 - core) + y * core
    t = y * (1 - core) + x * core

    def device(s_, t_):
        return ((t_ * RING + s_) * 2 * (1 - core) + ((s_ * RING + t_) * 2 + 1) * core, z)

    right_s, left_s, opp_s = lax.rem(s + 1, RING), lax.rem(s + 3, RING), lax.rem(s + 2, RING)
    right, left = device(right_s, t), device(left_s, t)
    partner = (past + 1 - 2 * core, z)
    t_of = [lax.rem(t + d, RING) for d in range(RING)]
    t_peer = [device(s, t_of[d]) for d in range(RING)]
    z_of = [lax.rem(z + d, n_z) for d in range(n_z)]
    z_peer = [(past, z_of[d]) for d in range(n_z)]

    loads = []

    def load(src, dst):
        copy = pltpu.make_async_copy(src, dst, load_sem.at[len(loads)])
        copy.start()
        loads.append(copy)
        return copy

    def sig_rows(b, part):
        return pl.ds(pl.multiple_of(b * rows + part * half, half), half)

    ld = {}
    ld["p0"] = load(sig_hbm.at[sig_rows(0, 1 - core)], sig.at[sig_rows(0, 1 - core)])
    ld["g0"] = load(g_hbm.at[:, 0:width], g.at[0])
    ld["o0"] = load(sig_hbm.at[sig_rows(0, core)], sig.at[sig_rows(0, core)])
    ld["g1"] = load(g_hbm.at[:, width : 2 * width], g.at[1])

    def load_rest():
        ld["p1"] = load(sig_hbm.at[sig_rows(1, 1 - core)], sig.at[sig_rows(1, 1 - core)])
        ld["o1"] = load(sig_hbm.at[sig_rows(1, core)], sig.at[sig_rows(1, core)])
        ld["edge"] = load(edge_hbm, edge)
        ld["vol"] = load(vol_hbm, vol)
        ld["coup"] = load(coup_hbm, coup)

    barrier = pltpu.get_barrier_semaphore()
    friends = [partner, right, left] + t_peer[1:] + z_peer[1:]
    for friend in friends:
        pl.semaphore_signal(barrier, inc=1, device_id=friend, device_id_type=MESH)

    sends = []
    ids = {}

    def sem_id(name):
        return ids.setdefault(name, len(ids))

    def put(name, src, dst, to):
        i = sem_id(name)
        copy = pltpu.make_async_remote_copy(
            src_ref=src, dst_ref=dst, send_sem=send_sem.at[i], recv_sem=recv_sem.at[i],
            device_id=to, device_id_type=MESH,
        )
        copy.start()
        sends.append(copy)

    def arrived(name, dst):
        i = sem_id(name)
        pltpu.make_async_remote_copy(
            src_ref=dst, dst_ref=dst, send_sem=send_sem.at[i], recv_sem=recv_sem.at[i],
            device_id=partner, device_id_type=MESH,
        ).wait_recv()

    def at(start, size):
        return pl.ds(pl.multiple_of(start, size), size)

    def product(k):
        b, j = k // 2, k % 2
        if j == 0:
            ld[f"p{b}"].wait()
        if b == 0:
            ld[f"g{j}"].wait()
        for i in range(width // tile):
            cols = pl.ds(i * tile, tile)
            psend[k, :, cols] = dot(sig[sig_rows(b, 1 - core)], g[j, :, cols]).astype(BF16)
        if k == 0:
            load_rest()
            pl.semaphore_wait(barrier, len(friends))
        put(("chip", k), psend.at[k], precv.at[k], partner)
        if j == 0:
            ld[f"o{b}"].wait()
        for i in range(width // tile):
            cols = pl.ds(i * tile, tile)
            own[k, :, cols] = dot(sig[sig_rows(b, core)], g[j, :, cols])

    def chip_sum(k):
        arrived(("chip", k), precv.at[k])
        a_buf[k] = (own[k] + precv[k].astype(F32)).astype(BF16)
        put(("a0", k), a_buf.at[k, at(opp_s * sub, hs)], ra.at[k, 0], right)
        put(("a1", k), a_buf.at[k, at(opp_s * sub + hs, hs)], ra.at[k, 1], left)
        put(("u0", k), a_buf.at[k, at(right_s * sub + hs, hs)], rb.at[k, 0, hs:sub], right)
        put(("u1", k), a_buf.at[k, at(left_s * sub, hs)], rb.at[k, 1, 0:hs], left)

    def ring_add(k):
        arrived(("a0", k), ra.at[k, 0])
        a2[k, 0] = (a_buf[k, at(right_s * sub, hs)].astype(F32) + ra[k, 0].astype(F32)).astype(BF16)
        put(("b0", k), a2.at[k, 0], rb.at[k, 0, 0:hs], right)
        arrived(("a1", k), ra.at[k, 1])
        a2[k, 1] = (a_buf[k, at(left_s * sub + hs, hs)].astype(F32) + ra[k, 1].astype(F32)).astype(BF16)
        put(("b1", k), a2.at[k, 1], rb.at[k, 1, hs:sub], left)

    def ring_sum(k):
        arrived(("u0", k), rb.at[k, 0, hs:sub])
        arrived(("u1", k), rb.at[k, 1, 0:hs])
        arrived(("b0", k), rb.at[k, 0, 0:hs])
        arrived(("b1", k), rb.at[k, 1, hs:sub])
        mine = at(s * sub, sub)
        total = (own[k, mine] + precv[k, mine].astype(F32)) + (rb[k, 0].astype(F32) + rb[k, 1].astype(F32))
        b_f32[k] = total
        b_buf[k] = total.astype(BF16)
        for d in range(1, RING):
            put(("c", k, d), b_buf.at[k, at(t_of[d] * piece, piece)], rc.at[k, d - 1], t_peer[d])

    def mem_at(k, part, s_, start, size):
        return mem.at[k, at(part * half + s_ * sub + start, size)]

    def piece_sum(k):
        total = b_f32[k, at(t * piece, piece)]
        for d in range(1, RING):
            arrived(("c", k, d), rc.at[k, d - 1])
            total = total + rc[k, d - 1].astype(F32)
        mem[k, at(core * half + s * sub + t * piece, piece)] = total.astype(BF16)
        for d in range(1, RING):
            ref = mem_at(k, core, s, t * piece, piece)
            put(("d", k, d), ref, ref, t_peer[d])

    def gather_first(k):
        for d in range(1, RING):
            arrived(("d", k, d), mem_at(k, core, s, t_of[RING - d] * piece, piece))
        ref = mem_at(k, core, s, 0, sub)
        put(("e0", k), ref, ref, right)
        put(("e1", k), ref, ref, left)
        put(("f0", k), ref, ref, partner)

    def gather_next(k):
        ref = mem_at(k, core, left_s, 0, sub)
        arrived(("e0", k), ref)
        low = mem_at(k, core, left_s, 0, hs)
        put(("h0", k), low, low, right)
        put(("f1", k), ref, ref, partner)
        ref = mem_at(k, core, right_s, 0, sub)
        arrived(("e1", k), ref)
        high = mem_at(k, core, right_s, hs, hs)
        put(("h1", k), high, high, left)
        put(("f2", k), ref, ref, partner)

    def gather_last(k):
        arrived(("h0", k), mem_at(k, core, opp_s, 0, hs))
        arrived(("h1", k), mem_at(k, core, opp_s, hs, hs))
        ref = mem_at(k, core, opp_s, 0, sub)
        put(("f3", k), ref, ref, partner)

    def gathered(k):
        arrived(("f0", k), mem_at(k, 1 - core, t, 0, sub))
        arrived(("f1", k), mem_at(k, 1 - core, t_of[3], 0, sub))
        arrived(("f2", k), mem_at(k, 1 - core, t_of[1], 0, sub))
        arrived(("f3", k), mem_at(k, 1 - core, t_of[2], 0, sub))

    def columns_of(k, i):
        return pl.ds((k % 2) * width + i * tile, tile)

    def fold(value):
        square = value * value
        part = jnp.sum(square.reshape(rows // 8, 8, tile), axis=0)
        out = part[:, 0:128]
        for i in range(1, tile // 128):
            out = out + part[:, i * 128 : (i + 1) * 128]
        return out

    def finish(b, cols, gnew):
        g_out[pl.ds(b * rows, rows), cols] = gnew.astype(BF16)
        cube = (gnew * gnew * gnew).reshape(rows // N, N, tile) * coup[:, cols][None]
        cube = cube.reshape(rows, tile)
        cubic[:, cols] = cube
        return fold(cube)

    def share(b, total):
        stat[b, z] = total
        for d in range(1, n_z):
            put(("z", b, d), stat.at[b, z], stat.at[b, z], z_peer[d])

    def scale_of(b):
        for d in range(1, n_z):
            arrived(("z", b, d), stat.at[b, z_of[n_z - d]])
        total = jnp.sum(jnp.sum(stat[b], axis=0))
        mean = total / count_all
        return jnp.sqrt(jnp.full((8, 128), mean + 1e-6, F32))[0:1, 0:1]

    def scaled(b, scale):
        inv = 1.0 / scale
        for i in range(2 * width // tile):
            cols = pl.ds(i * tile, tile)
            s_out[pl.ds(b * rows, rows), cols] = (cubic[:, cols] * inv).astype(BF16)

    def start_value():
        ld["edge"].wait()
        ld["vol"].wait()
        ld["coup"].wait()
        for i in range(2 * width // tile):
            cols = pl.ds(i * tile, tile)
            s_buf[0, :, cols] = dot(vol[0, :, rows : 2 * rows], edge[:, cols])

    def first_block(k):
        gathered(k)
        total = None
        for i in range(width // tile):
            cols = columns_of(k, i)
            gnew = s_buf[0, :, cols] + dot(vol[0, :, 0:rows], mem[k, :, pl.ds(i * tile, tile)])
            part = finish(0, cols, gnew)
            total = part if total is None else total + part
        return total

    def second_memory(k):
        gathered(k)
        for i in range(width // tile):
            s_buf[1, :, columns_of(k, i)] = dot(vol[1, :, 0:rows], mem[k, :, pl.ds(i * tile, tile)])

    stages = [chip_sum, ring_add, ring_sum, piece_sum, gather_first, gather_next, gather_last]
    sums = []
    for step in range(CHUNKS + len(stages) + 1):
        if step < CHUNKS:
            product(step)
        if step == CHUNKS:
            start_value()
        for k in range(CHUNKS):
            i = step - k - 1
            if 0 <= i < len(stages):
                stages[i](k)
            if i == len(stages):
                if k < 2:
                    sums.append(first_block(k))
                    if k == 1:
                        share(0, sums[0] + sums[1])
                else:
                    second_memory(k)

    scaled(0, scale_of(0))
    total = None
    for i in range(2 * width // tile):
        cols = pl.ds(i * tile, tile)
        gnew = s_buf[1, :, cols] + dot(vol[1, :, rows : 2 * rows], s_out[0:rows, cols])
        part = finish(1, cols, gnew)
        total = part if total is None else total + part
    share(1, total)
    scaled(1, scale_of(1))
    for copy in sends:
        copy.wait_send()


def per_device(g_hist, sigma_hist, volterra, sigma_edge, coupling):
    rows = volterra.shape[1]
    columns = g_hist.shape[1]
    depth = g_hist.shape[0]
    n_z = lax.axis_size("second")
    width = columns // 2
    half = rows // 2
    sub = half // RING
    piece = sub // RING
    n_sem = 21 * CHUNKS + 2 * (n_z - 1)
    vmem = pltpu.VMEM
    return pl.pallas_call(
        functools.partial(kernel, n_z, rows * columns * n_z),
        out_shape=[jax.ShapeDtypeStruct((2 * rows, columns), BF16)] * 2,
        in_specs=[pl.BlockSpec(memory_space=pl.ANY)] * 5,
        out_specs=[pl.BlockSpec(memory_space=pltpu.VMEM)] * 2,
        scratch_shapes=[
            vmem((2, depth, width), BF16),
            vmem((2 * rows, depth), BF16),
            vmem(volterra.shape, BF16),
            vmem(sigma_edge.shape, BF16),
            vmem(coupling.shape, F32),
            vmem((CHUNKS, half, width), BF16),
            vmem((CHUNKS, half, width), BF16),
            vmem((CHUNKS, half, width), F32),
            vmem((CHUNKS, half, width), BF16),
            vmem((CHUNKS, 2, sub // 2, width), BF16),
            vmem((CHUNKS, 2, sub // 2, width), BF16),
            vmem((CHUNKS, 2, sub, width), BF16),
            vmem((CHUNKS, sub, width), BF16),
            vmem((CHUNKS, sub, width), F32),
            vmem((CHUNKS, RING - 1, piece, width), BF16),
            vmem((CHUNKS, rows, width), BF16),
            vmem((2, rows, columns), F32),
            vmem((rows, columns), F32),
            vmem((2, n_z, 8, 128), F32),
            pltpu.SemaphoreType.DMA((n_sem,)),
            pltpu.SemaphoreType.DMA((n_sem,)),
            pltpu.SemaphoreType.DMA((9,)),
        ],
        compiler_params=pltpu.CompilerParams(
            collective_id=0, has_side_effects=True, vmem_limit_bytes=60 * 1024 * 1024
        ),
    )(g_hist, sigma_hist, volterra, sigma_edge, coupling)


def solution(mesh):
    return jax.shard_map(
        per_device,
        mesh=mesh,
        in_specs=(P("past", "second"), P(None, "past"), P(), P(None, "second"), P(None, "second")),
        out_specs=(P(None, "second"), P(None, "second")),
        check_vma=False,
    )
```

time: 329 us -> 62.8 us (0.19)
  waiting for transfers between devices: 242 us -> 0 us
  Pallas kernels: 0 us -> 57.5 us
  blocking collectives: 29.1 us -> 0 us
  matrix products: 23.6 us -> 0 us
  between operations: 15.2 us -> 0.65 us
  other arithmetic: 11.2 us -> 0 us
    reduce_scatter x2 -> x0, waiting for transfers between devices: 171 us -> none  [per_device(): lax.psum_scatter(jnp.dot(sig_rows, g_hist, preferred_element_type=jnp.flo...]
    all_gather x2 -> x0, waiting for transfers between devices: 71.2 us -> none  [per_device(): lax.all_gather(mine, 'past', axis=0, tiled=True)]
    pallas_call x0 -> x1, Pallas kernels: none -> 57.5 us  [per_device(): pl.pallas_call(functools.partial(kernel, n_z, rows * columns * n_z), out_...]
    psum x2 -> x0, blocking collectives: 29.1 us -> none  [per_device(): total_sq = lax.psum(local_sq, 'second')]
    dot_general x6 -> x0, matrix products: 23.6 us -> none  [the longest x2 13 us: per_device(): jnp.dot(sig_rows, g_hist, preferred_element_type=jnp.float32)]
    convert_element_type x4 -> x0, other arithmetic: 7.04 us -> none  [the longest x1 3.79 us: per_device(): g_blocks.append(gnew.astype(jnp.bfloat16))]
  transfers between devices with their start and end apart: 4 -> 0, of which waited for: 4 -> 0; matrix products, arithmetic and copies ran while one was open for 6% -> 0% of each run, Pallas kernels for 0% -> 0%
where the time goes in v1:
time: 62.8 us; the launch traced here: 62.7 us
  Pallas kernels  57.5 us (92%)
  local copies, waits for them, and re-layouts  4.55 us (7%)
  between operations  0.65 us (1%)
    pallas_call x1, Pallas kernels, per_device(): pl.pallas_call(functools.partial(kernel, n_z, rows * columns * n_z), out_...  57.5 us
    unnamed x4, local copies, waits for them, and re-layouts  4.55 us

profile of v1, /device:TPU:1, one launch (start us, length us, event | category | flops | bytes accessed | tf_op | source)
XLA Modules:
  0.0 62.7 jit_solution(1524036063877188903)
XLA Ops:
  0.6 57.5 %shard_map.68 = (bf16[1024,1024]{1,0:T(8,128)(2,1)}, bf16[1024,1024]{1,0:T(8,128)(2,1)}) custom-call(bf16[2048,1024]{1,0:T(8,128)(2,1)} %g_hbm.1, bf16[1024,2048]{1,0:T(8,128)(2,1)} %sig_hbm.1, bf16[2,512,1024]{2,1,0:T(8,128)(2,1)} %vol_hbm.1, bf16[512,1024]{1,0:T(8,128)(2,1)} %edge_hbm.1, f32[32,1024]{1,0:T(8,128)} %coup_hbm.1), custom_call_target="tpu_custom_call" | custom-call | tf_op jit(solution)/shard_map/pallas_call | solution.py:303
  58.1 0.0 copy-start
  58.1 3.2 %copy.9 = bf16[1024,1024]{1,0:T(8,128)(2,1)} copy(bf16[1024,1024]{1,0:T(8,128)(2,1)} %get-tuple-element.4) | data formatting | bytes 4194304
  61.4 0.0 copy-done
  61.4 1.3 %copy.10 = bf16[1024,1024]{1,0:T(8,128)(2,1)} copy(bf16[1024,1024]{1,0:T(8,128)(2,1)S(1)} %copy-done) | data formatting | bytes 4194304
Async XLA Ops:
  58.1 3.2 %copy-start = (bf16[1024,1024]{1,0:T(8,128)(2,1)S(1)}, bf16[1024,1024]{1,0:T(8,128)(2,1)}, u32[]{:S(2)}) copy-start(bf16[1024,1024]{1,0:T(8,128)(2,1)} %get-tuple-element.5) | copy-start | bytes 6291460

commit v2 on v1

v2 whole, which is shorter than its diff:
```python
import functools

import jax
import jax.numpy as jnp
from jax import lax
from jax.experimental import pallas as pl
from jax.experimental.pallas import tpu as pltpu
from jax.sharding import PartitionSpec as P

N = 32
MESH = pl.DeviceIdType.MESH
F32 = jnp.float32
BF16 = jnp.bfloat16
RING = 4
CHUNKS = 4


def dot(a, b):
    return jnp.dot(a, b, preferred_element_type=F32)


def kernel(
    n_z, count_all,
    g_hbm, sig_hbm, vol_hbm, edge_hbm, coup_hbm, g_out, s_out,
    g, sig, vol, edge, coup, psend, precv, own, a_buf, ra, b_buf, mem, s_buf, cubic, stat,
    send_sem, recv_sem, load_sem,
):
    rows = mem.shape[1]
    half = rows // 2
    sub = half // RING
    width = mem.shape[2]
    tile = min(256, width)

    past = lax.axis_index("past")
    z = lax.axis_index("second")
    core = lax.rem(past, 2)
    x = lax.rem(past // 2, RING)
    y = past // (2 * RING)
    partner = (past + 1 - 2 * core, z)
    x_of = [lax.rem(x + d, RING) for d in range(RING)]
    y_of = [lax.rem(y + d, RING) for d in range(RING)]
    x_peer = [((y * RING + x_of[d]) * 2 + core, z) for d in range(RING)]
    y_peer = [((y_of[d] * RING + x) * 2 + core, z) for d in range(RING)]
    s_of, t_of = [x_of, y_of], [y_of, x_of]
    s_peer, t_peer = [x_peer, y_peer], [y_peer, x_peer]
    z_of = [lax.rem(z + d, n_z) for d in range(n_z)]
    z_peer = [(past, z_of[d]) for d in range(n_z)]

    loads = []

    def load(src, dst):
        copy = pltpu.make_async_copy(src, dst, load_sem.at[len(loads)])
        copy.start()
        loads.append(copy)
        return copy

    def sig_rows(b, part):
        return pl.ds(pl.multiple_of(b * rows + part * half, half), half)

    ld = {}
    ld["p0"] = load(sig_hbm.at[sig_rows(0, 1 - core)], sig.at[sig_rows(0, 1 - core)])
    ld["g0"] = load(g_hbm.at[:, 0:width], g.at[0])
    ld["o0"] = load(sig_hbm.at[sig_rows(0, core)], sig.at[sig_rows(0, core)])
    ld["g1"] = load(g_hbm.at[:, width : 2 * width], g.at[1])

    def load_rest():
        ld["p1"] = load(sig_hbm.at[sig_rows(1, 1 - core)], sig.at[sig_rows(1, 1 - core)])
        ld["o1"] = load(sig_hbm.at[sig_rows(1, core)], sig.at[sig_rows(1, core)])
        ld["edge"] = load(edge_hbm, edge)
        ld["vol"] = load(vol_hbm, vol)
        ld["coup"] = load(coup_hbm, coup)

    barrier = pltpu.get_barrier_semaphore()
    friends = [partner] + x_peer[1:] + y_peer[1:] + z_peer[1:]
    for friend in friends:
        pl.semaphore_signal(barrier, inc=1, device_id=friend, device_id_type=MESH)

    sends = []
    ids = {}

    def sem_id(name):
        return ids.setdefault(name, len(ids))

    def put(name, src, dst, to):
        i = sem_id(name)
        copy = pltpu.make_async_remote_copy(
            src_ref=src, dst_ref=dst, send_sem=send_sem.at[i], recv_sem=recv_sem.at[i],
            device_id=to, device_id_type=MESH,
        )
        copy.start()
        sends.append(copy)

    def arrived(name, dst):
        i = sem_id(name)
        pltpu.make_async_remote_copy(
            src_ref=dst, dst_ref=dst, send_sem=send_sem.at[i], recv_sem=recv_sem.at[i],
            device_id=partner, device_id_type=MESH,
        ).wait_recv()

    def at(start, size):
        return pl.ds(pl.multiple_of(start, size), size)

    def product_send(k):
        b, j = k // 2, k % 2
        if j == 0:
            ld[f"p{b}"].wait()
        if b == 0:
            ld[f"g{j}"].wait()
        for i in range(width // tile):
            cols = pl.ds(i * tile, tile)
            psend[k, :, cols] = dot(sig[sig_rows(b, 1 - core)], g[j, :, cols])
        if k == 0:
            load_rest()
            pl.semaphore_wait(barrier, len(friends))
        put(("chip", k), psend.at[k], precv.at[k], partner)

    def product_own(k):
        b, j = k // 2, k % 2
        if j == 0:
            ld[f"o{b}"].wait()
        for i in range(width // tile):
            cols = pl.ds(i * tile, tile)
            own[k, :, cols] = dot(sig[sig_rows(b, core)], g[j, :, cols])

    def mine(k):
        return at(s_of[k % 2][0] * sub, sub)

    def chip_sum(k):
        arrived(("chip", k), precv.at[k])
        a_buf[k] = (own[k] + precv[k]).astype(BF16)
        for d in (2, 1, 3):
            put(("a", k, d), a_buf.at[k, at(s_of[k % 2][d] * sub, sub)], ra.at[k, d - 1], s_peer[k % 2][d])

    def ring_sum(k):
        t = t_of[k % 2]
        total = own[k, mine(k)] + precv[k, mine(k)]
        for d in (1, 3, 2):
            arrived(("a", k, d), ra.at[k, d - 1])
            total = total + ra[k, d - 1].astype(F32)
        b_buf[k, t[0]] = total.astype(BF16)
        for d in (2, 1, 3):
            put(("b", k, d), b_buf.at[k, t[0]], b_buf.at[k, t[0]], t_peer[k % 2][d])

    def mem_at(k, part, d):
        return mem.at[k, at(part * half + s_of[k % 2][d] * sub, sub)]

    def plane_sum(k):
        t = t_of[k % 2]
        for d in (1, 3, 2):
            arrived(("b", k, d), b_buf.at[k, t[RING - d]])
        total = b_buf[k, 0].astype(F32)
        for i in range(1, RING):
            total = total + b_buf[k, i].astype(F32)
        mem[k, at(core * half + s_of[k % 2][0] * sub, sub)] = total.astype(BF16)
        ref = mem_at(k, core, 0)
        for d in (2, 1, 3):
            put(("c", k, d), ref, ref, s_peer[k % 2][d])
        put(("f", k, 0), ref, ref, partner)

    def gather(k):
        for d in (1, 3, 2):
            ref = mem_at(k, core, RING - d)
            arrived(("c", k, d), ref)
            put(("f", k, RING - d), ref, ref, partner)

    def gathered(k):
        for d in (0, 3, 1, 2):
            arrived(("f", k, d), mem_at(k, 1 - core, d))

    def columns_of(k, i):
        return pl.ds((k % 2) * width + i * tile, tile)

    def fold(value):
        square = value * value
        part = jnp.sum(square.reshape(rows // 8, 8, tile), axis=0)
        out = part[:, 0:128]
        for i in range(1, tile // 128):
            out = out + part[:, i * 128 : (i + 1) * 128]
        return out

    def finish(b, cols, gnew):
        g_out[pl.ds(b * rows, rows), cols] = gnew.astype(BF16)
        cube = (gnew * gnew * gnew).reshape(rows // N, N, tile) * coup[:, cols][None]
        cube = cube.reshape(rows, tile)
        cubic[:, cols] = cube
        return fold(cube)

    def share(b, total):
        stat[b, z] = total
        for d in range(1, n_z):
            put(("z", b, d), stat.at[b, z], stat.at[b, z], z_peer[d])

    def scale_of(b):
        for d in range(1, n_z):
            arrived(("z", b, d), stat.at[b, z_of[n_z - d]])
        total = jnp.sum(jnp.sum(stat[b], axis=0))
        mean = total / count_all
        return jnp.sqrt(jnp.full((8, 128), mean + 1e-6, F32))[0:1, 0:1]

    def scaled(b, scale):
        inv = 1.0 / scale
        for i in range(2 * width // tile):
            cols = pl.ds(i * tile, tile)
            s_out[pl.ds(b * rows, rows), cols] = (cubic[:, cols] * inv).astype(BF16)

    def start_value():
        ld["edge"].wait()
        ld["vol"].wait()
        ld["coup"].wait()
        for i in range(2 * width // tile):
            cols = pl.ds(i * tile, tile)
            s_buf[0, :, cols] = dot(vol[0, :, rows : 2 * rows], edge[:, cols])

    def first_block(k):
        gathered(k)
        total = None
        for i in range(width // tile):
            cols = columns_of(k, i)
            gnew = s_buf[0, :, cols] + dot(vol[0, :, 0:rows], mem[k, :, pl.ds(i * tile, tile)])
            part = finish(0, cols, gnew)
            total = part if total is None else total + part
        return total

    def second_memory(k):
        gathered(k)
        for i in range(width // tile):
            s_buf[1, :, columns_of(k, i)] = dot(vol[1, :, 0:rows], mem[k, :, pl.ds(i * tile, tile)])

    product_send(0)
    product_own(0)
    for k in range(1, CHUNKS):
        product_send(k)
        chip_sum(k - 1)
        product_own(k)
    chip_sum(CHUNKS - 1)
    start_value()
    ring_sum(0)
    ring_sum(1)
    ring_sum(2)
    plane_sum(0)
    ring_sum(3)
    plane_sum(1)
    plane_sum(2)
    gather(0)
    plane_sum(3)
    gather(1)
    total = first_block(0)
    gather(2)
    total = total + first_block(1)
    share(0, total)
    gather(3)
    second_memory(2)
    second_memory(3)

    scaled(0, scale_of(0))
    total = None
    for i in range(2 * width // tile):
        cols = pl.ds(i * tile, tile)
        gnew = s_buf[1, :, cols] + dot(vol[1, :, rows : 2 * rows], s_out[0:rows, cols])
        part = finish(1, cols, gnew)
        total = part if total is None else total + part
    share(1, total)
    scaled(1, scale_of(1))
    for copy in sends:
        copy.wait_send()


def per_device(g_hist, sigma_hist, volterra, sigma_edge, coupling):
    rows = volterra.shape[1]
    columns = g_hist.shape[1]
    depth = g_hist.shape[0]
    n_z = lax.axis_size("second")
    width = columns // 2
    half = rows // 2
    sub = half // RING
    n_sem = 14 * CHUNKS + 2 * (n_z - 1)
    vmem = pltpu.VMEM
    return pl.pallas_call(
        functools.partial(kernel, n_z, rows * columns * n_z),
        out_shape=[pltpu.VMEM((2 * rows, columns), BF16)] * 2,
        in_specs=[pl.BlockSpec(memory_space=pltpu.HBM)] * 5,
        out_specs=[pl.BlockSpec(memory_space=pltpu.VMEM)] * 2,
        scratch_shapes=[
            vmem((2, depth, width), BF16),
            vmem((2 * rows, depth), BF16),
            vmem(volterra.shape, BF16),
            vmem(sigma_edge.shape, BF16),
            vmem(coupling.shape, F32),
            vmem((CHUNKS, half, width), F32),
            vmem((CHUNKS, half, width), F32),
            vmem((CHUNKS, half, width), F32),
            vmem((CHUNKS, half, width), BF16),
            vmem((CHUNKS, RING - 1, sub, width), BF16),
            vmem((CHUNKS, RING, sub, width), BF16),
            vmem((CHUNKS, rows, width), BF16),
            vmem((2, rows, columns), F32),
            vmem((rows, columns), F32),
            vmem((2, n_z, 8, 128), F32),
            pltpu.SemaphoreType.DMA((n_sem,)),
            pltpu.SemaphoreType.DMA((n_sem,)),
            pltpu.SemaphoreType.DMA((9,)),
        ],
        compiler_params=pltpu.CompilerParams(
            collective_id=0, has_side_effects=True, vmem_limit_bytes=62_800_000
        ),
    )(g_hist, sigma_hist, volterra, sigma_edge, coupling)


def solution(mesh):
    return jax.shard_map(
        per_device,
        mesh=mesh,
        in_specs=(P("past", "second"), P(None, "past"), P(), P(None, "second"), P(None, "second")),
        out_specs=(P(None, "second"), P(None, "second")),
        check_vma=False,
    )
```

time: 62.8 us -> 50.7 us (0.81)
  Pallas kernels: 57.5 us -> 47.3 us
  local copies, waits for them, and re-layouts: 4.55 us -> 2.64 us
    pallas_call x1, Pallas kernels: 57.5 us -> 47.3 us  [per_device(): pl.pallas_call(functools.partial(kernel, n_z, rows * columns * n_z), out_...]
    unnamed x4 -> x2, local copies, waits for them, and re-layouts: 4.55 us -> 2.64 us
where the time goes in v2:
time: 50.7 us; the launch traced here: 50.6 us
  Pallas kernels  47.3 us (93%)
  local copies, waits for them, and re-layouts  2.64 us (5%)
  between operations  0.64 us (1%)
    pallas_call x1, Pallas kernels, per_device(): pl.pallas_call(functools.partial(kernel, n_z, rows * columns * n_z), out_...  47.3 us
    unnamed x2, local copies, waits for them, and re-layouts  2.64 us

profile of v2, /device:TPU:1, one launch (start us, length us, event | category | flops | bytes accessed | tf_op | source)
XLA Modules:
  0.0 50.6 jit_solution(11018549607776027347)
XLA Ops:
  0.6 47.3 %shard_map.68 = (bf16[1024,1024]{1,0:T(8,128)(2,1)S(1)}, bf16[1024,1024]{1,0:T(8,128)(2,1)S(1)}) custom-call(bf16[2048,1024]{1,0:T(8,128)(2,1)} %g_hbm.1, bf16[1024,2048]{1,0:T(8,128)(2,1)} %sig_hbm.1, bf16[2,512,1024]{2,1,0:T(8,128)(2,1)} %vol_hbm.1, bf16[512,1024]{1,0:T(8,128)(2,1)} %edge_hbm.1, f32[32,1024]{1,0:T(8,128)} %coup_hbm.1), custom_call_target="tpu_custom_call" | custom-call | tf_op jit(solution)/shard_map/pallas_call | solution.py:278
  48.0 1.3 %copy.9 = bf16[1024,1024]{1,0:T(8,128)(2,1)} copy(bf16[1024,1024]{1,0:T(8,128)(2,1)S(1)} %get-tuple-element.2) | data formatting | bytes 4194304
  49.3 1.3 %copy.10 = bf16[1024,1024]{1,0:T(8,128)(2,1)} copy(bf16[1024,1024]{1,0:T(8,128)(2,1)S(1)} %get-tuple-element.3) | data formatting | bytes 4194304

commit v3 on v2

v3 whole, which is shorter than its diff:
```python
import functools

import jax
import jax.numpy as jnp
from jax import lax
from jax.experimental import pallas as pl
from jax.experimental.pallas import tpu as pltpu
from jax.sharding import PartitionSpec as P

N = 32
MESH = pl.DeviceIdType.MESH
F32 = jnp.float32
BF16 = jnp.bfloat16
RING = 4
CHUNKS = 4


def dot(a, b):
    return jnp.dot(a, b, preferred_element_type=F32)


def kernel(
    n_z, count_all,
    g_hbm, sig_hbm, vol_hbm, edge_hbm, coup_hbm, g_out, s_out,
    g, sig, vol, edge, coup, psend, precv, own, a_buf, ra, b_buf, mem, s_buf, cubic0, cubic, cube16, stat,
    send_sem, recv_sem, load_sem,
):
    rows = mem.shape[1]
    half = rows // 2
    sub = half // 2 // RING
    width = mem.shape[2]
    tile = min(256, width)

    past = lax.axis_index("past")
    z = lax.axis_index("second")
    core = lax.rem(past, 2)
    x = lax.rem(past // 2, RING)
    y = past // (2 * RING)
    partner = (past + 1 - 2 * core, z)
    def bits(p):
        return lax.rem((p + 1) // 2, 2), p // 2

    xi, xj = bits(x)
    yi, yj = bits(y)

    def flip(bit, yes):
        return 1 - bit if yes else bit

    def position(i, j):
        return i + j * (3 - 2 * i)

    def face_of(f, d):
        dx, dy = d % 2, d // 2
        if f == 0:
            bx, by = flip(xi, dx), flip(yi, dy)
            px, py = position(bx, xj), position(by, yj)
        else:
            bx, by = flip(xj, dx), flip(yj, dy)
            px, py = position(xi, bx), position(yi, by)
        return bx + 2 * by, ((py * RING + px) * 2 + core, z)

    faces = [[face_of(f, d) for d in range(RING)] for f in range(2)]
    s_of = [[faces[f][d][0] for d in range(RING)] for f in (0, 1)]
    t_of = [s_of[1], s_of[0]]
    s_peer = [[faces[f][d][1] for d in range(RING)] for f in (0, 1)]
    t_peer = [s_peer[1], s_peer[0]]
    z_of = [lax.rem(z + d, n_z) for d in range(n_z)]
    z_peer = [(past, z_of[d]) for d in range(n_z)]

    loads = []

    def load(src, dst):
        copy = pltpu.make_async_copy(src, dst, load_sem.at[len(loads)])
        copy.start()
        loads.append(copy)
        return copy

    def sig_rows(b, part):
        return pl.ds(pl.multiple_of(b * rows + part * half, half), half)

    ld = {}
    ld["p0"] = load(sig_hbm.at[sig_rows(0, 1 - core)], sig.at[sig_rows(0, 1 - core)])
    first = [load(g_hbm.at[:, i * tile : (i + 1) * tile], g.at[0, :, i * tile : (i + 1) * tile]) for i in range(width // tile)]

    def load_more():
        ld["o0"] = load(sig_hbm.at[sig_rows(0, core)], sig.at[sig_rows(0, core)])
        ld["g1"] = load(g_hbm.at[:, width : 2 * width], g.at[1])

    def load_rest():
        ld["p1"] = load(sig_hbm.at[sig_rows(1, 1 - core)], sig.at[sig_rows(1, 1 - core)])
        ld["o1"] = load(sig_hbm.at[sig_rows(1, core)], sig.at[sig_rows(1, core)])
        ld["edge"] = load(edge_hbm, edge)
        ld["vol"] = load(vol_hbm, vol)
        ld["coup"] = load(coup_hbm, coup)

    barrier = pltpu.get_barrier_semaphore()
    friends = [partner] + s_peer[0][1:] + s_peer[1][1:] + z_peer[1:]
    for friend in friends:
        pl.semaphore_signal(barrier, inc=1, device_id=friend, device_id_type=MESH)

    sends = []
    ids = {}

    def sem_id(name):
        return ids.setdefault(name, len(ids))

    def put(name, src, dst, to):
        i = sem_id(name)
        copy = pltpu.make_async_remote_copy(
            src_ref=src, dst_ref=dst, send_sem=send_sem.at[i], recv_sem=recv_sem.at[i],
            device_id=to, device_id_type=MESH,
        )
        copy.start()
        sends.append(copy)

    def arrived(name, dst):
        i = sem_id(name)
        pltpu.make_async_remote_copy(
            src_ref=dst, dst_ref=dst, send_sem=send_sem.at[i], recv_sem=recv_sem.at[i],
            device_id=partner, device_id_type=MESH,
        ).wait_recv()

    def at(start, size):
        return pl.ds(pl.multiple_of(start, size), size)

    def product_send(k):
        b, j = k // 2, k % 2
        if j == 0:
            ld[f"p{b}"].wait()
        if k == 0:
            load_more()
        if k == 1:
            ld["g1"].wait()
        for i in range(width // tile):
            if k == 0:
                first[i].wait()
            cols = pl.ds(i * tile, tile)
            psend[k, :, cols] = dot(sig[sig_rows(b, 1 - core)], g[j, :, cols])
        if k == 0:
            load_rest()
            pl.semaphore_wait(barrier, len(friends))
        put(("chip", k), psend.at[k], precv.at[k], partner)

    def product_own(k):
        b, j = k // 2, k % 2
        if j == 0:
            ld[f"o{b}"].wait()
        for i in range(width // tile):
            cols = pl.ds(i * tile, tile)
            own[k, :, cols] = dot(sig[sig_rows(b, core)], g[j, :, cols])

    def row(h, d):
        return pl.multiple_of(h * (half // 2) + s_of[h][d] * sub, sub)

    def chip_sum(k):
        arrived(("chip", k), precv.at[k])
        a_buf[k] = (own[k] + precv[k]).astype(BF16)
        for d in (3, 1, 2):
            for h in range(2):
                put(("a", k, h, d), a_buf.at[k, pl.ds(row(h, d), sub)], ra.at[k, h, d - 1], s_peer[h][d])

    def ring_sum(k):
        for h in range(2):
            mine = pl.ds(row(h, 0), sub)
            t = t_of[h]
            total = own[k, mine] + precv[k, mine]
            for d in (2, 1, 3):
                arrived(("a", k, h, d), ra.at[k, h, d - 1])
                total = total + ra[k, h, d - 1].astype(F32)
            b_buf[k, h, t[0]] = total.astype(BF16)
            for d in (3, 1, 2):
                ref = b_buf.at[k, h, t[0]]
                put(("b", k, h, d), ref, ref, t_peer[h][d])

    def mem_at(k, part, h, d):
        return mem.at[k, pl.ds(pl.multiple_of(part * half + row(h, d), sub), sub)]

    def plane_sum(k):
        for h in range(2):
            for d in (2, 1, 3):
                arrived(("b", k, h, d), b_buf.at[k, h, t_of[h][d]])
            total = b_buf[k, h, 0].astype(F32)
            for i in range(1, RING):
                total = total + b_buf[k, h, i].astype(F32)
            mem[k, pl.ds(pl.multiple_of(core * half + row(h, 0), sub), sub)] = total.astype(BF16)
            ref = mem_at(k, core, h, 0)
            for d in (3, 1, 2):
                put(("c", k, h, d), ref, ref, s_peer[h][d])
            put(("f", k, h, 0), ref, ref, partner)

    def gather(k):
        for d in (2, 1, 3):
            for h in range(2):
                ref = mem_at(k, core, h, d)
                arrived(("c", k, h, d), ref)
                put(("f", k, h, d), ref, ref, partner)

    def gathered(k):
        for d in (0, 2, 1, 3):
            for h in range(2):
                arrived(("f", k, h, d), mem_at(k, 1 - core, h, d))

    def columns_of(k, i):
        return pl.ds((k % 2) * width + i * tile, tile)

    def fold(value):
        square = value * value
        part = jnp.sum(square.reshape(rows // 8, 8, tile), axis=0)
        out = part[:, 0:128]
        for i in range(1, tile // 128):
            out = out + part[:, i * 128 : (i + 1) * 128]
        return out

    def cube_of(cols, gnew):
        cube = (gnew * gnew * gnew).reshape(rows // N, N, tile) * coup[:, cols][None]
        return cube.reshape(rows, tile)

    def finish(cols, gnew):
        cube = cube_of(cols, gnew)
        cubic[:, cols] = cube
        return fold(cube)

    def share(b, total):
        stat[b, z] = total
        for d in range(1, n_z):
            put(("z", b, d), stat.at[b, z], stat.at[b, z], z_peer[d])

    def scale_of(b):
        for d in range(1, n_z):
            arrived(("z", b, d), stat.at[b, z_of[n_z - d]])
        total = jnp.sum(jnp.sum(stat[b], axis=0))
        mean = total / count_all
        return jnp.sqrt(jnp.full((8, 128), mean + 1e-6, F32))[0:1, 0:1]

    def start_value(i):
        if i == 0:
            ld["edge"].wait()
            ld["vol"].wait()
            ld["coup"].wait()
        cols = pl.ds(i * width // 2, width // 2)
        s_buf[0, :, cols] = dot(vol[0, :, rows : 2 * rows], edge[:, cols])

    def first_block(k):
        gathered(k)
        total = None
        for i in range(width // tile):
            cols = columns_of(k, i)
            gnew = s_buf[0, :, cols] + dot(vol[0, :, 0:rows], mem[k, :, pl.ds(i * tile, tile)])
            cube = cube_of(cols, gnew)
            cubic0[:, cols] = cube
            cube16[:, cols] = cube.astype(BF16)
            g_out[0:rows, cols] = gnew.astype(BF16)
            part = fold(cube)
            total = part if total is None else total + part
        return total

    def second_memory(k):
        gathered(k)
        for i in range(width // tile):
            s_buf[1, :, columns_of(k, i)] = dot(vol[1, :, 0:rows], mem[k, :, pl.ds(i * tile, tile)])

    product_send(0)
    product_own(0)
    for k in range(1, CHUNKS):
        product_send(k)
        chip_sum(k - 1)
        product_own(k)
    ring_sum(0)
    chip_sum(3)
    start_value(0)
    ring_sum(1)
    start_value(1)
    ring_sum(2)
    start_value(2)
    plane_sum(0)
    ring_sum(3)
    start_value(3)
    plane_sum(1)
    plane_sum(2)
    gather(0)
    plane_sum(3)
    gather(1)
    total = first_block(0)
    total = total + first_block(1)
    share(0, total)
    gather(2)
    gather(3)
    for i in range(2 * width // tile):
        cols = pl.ds(i * tile, tile)
        s_buf[0, :, cols] = dot(vol[1, :, rows : 2 * rows], cube16[:, cols])
    second_memory(2)
    second_memory(3)
    inv0 = 1.0 / scale_of(0)
    total = None
    for i in range(2 * width // tile):
        cols = pl.ds(i * tile, tile)
        gnew = s_buf[1, :, cols] + s_buf[0, :, cols] * inv0
        s_buf[1, :, cols] = gnew
        part = finish(cols, gnew)
        total = part if total is None else total + part
    share(1, total)
    for i in range(2 * width // tile):
        cols = pl.ds(i * tile, tile)
        g_out[rows : 2 * rows, cols] = s_buf[1, :, cols].astype(BF16)
        s_out[0:rows, cols] = (cubic0[:, cols] * inv0).astype(BF16)
    inv1 = 1.0 / scale_of(1)
    for i in range(2 * width // tile):
        cols = pl.ds(i * tile, tile)
        s_out[rows : 2 * rows, cols] = (cubic[:, cols] * inv1).astype(BF16)
    for copy in sends:
        copy.wait_send()


def write_out(g_in, s_in, g_out, s_out, sem):
    part = g_in.shape[0] // 4
    copies = []
    for i in range(4):
        for a, (src, dst) in enumerate(((g_in, g_out), (s_in, s_out))):
            here = pl.ds(i * part, part)
            copies.append(pltpu.make_async_copy(src.at[here], dst.at[here], sem.at[2 * i + a]))
            copies[-1].start()
    for copy in copies:
        copy.wait()


def per_device(g_hist, sigma_hist, volterra, sigma_edge, coupling):
    rows = volterra.shape[1]
    columns = g_hist.shape[1]
    depth = g_hist.shape[0]
    n_z = lax.axis_size("second")
    width = columns // 2
    half = rows // 2
    sub = half // 2 // RING
    n_sem = 27 * CHUNKS + 2 * (n_z - 1)
    vmem = pltpu.VMEM
    outs = pl.pallas_call(
        functools.partial(kernel, n_z, rows * columns * n_z),
        out_shape=[pltpu.VMEM((2 * rows, columns), BF16)] * 2,
        in_specs=[pl.BlockSpec(memory_space=pltpu.HBM)] * 5,
        out_specs=[pl.BlockSpec(memory_space=pltpu.VMEM)] * 2,
        scratch_shapes=[
            vmem((2, depth, width), BF16),
            vmem((2 * rows, depth), BF16),
            vmem(volterra.shape, BF16),
            vmem(sigma_edge.shape, BF16),
            vmem(coupling.shape, F32),
            vmem((CHUNKS, half, width), F32),
            vmem((CHUNKS, half, width), F32),
            vmem((CHUNKS, half, width), F32),
            vmem((CHUNKS, half, width), BF16),
            vmem((CHUNKS, 2, RING - 1, sub, width), BF16),
            vmem((CHUNKS, 2, RING, sub, width), BF16),
            vmem((CHUNKS, rows, width), BF16),
            vmem((2, rows, columns), F32),
            vmem((rows, columns), F32),
            vmem((rows, columns), F32),
            vmem((rows, columns), BF16),
            vmem((2, n_z, 8, 128), F32),
            pltpu.SemaphoreType.DMA((n_sem,)),
            pltpu.SemaphoreType.DMA((n_sem,)),
            pltpu.SemaphoreType.DMA((10,)),
        ],
        compiler_params=pltpu.CompilerParams(
            collective_id=0, has_side_effects=True, vmem_limit_bytes=62_800_000
        ),
    )(g_hist, sigma_hist, volterra, sigma_edge, coupling)
    return pl.pallas_call(
        write_out,
        out_shape=[jax.ShapeDtypeStruct((2 * rows, columns), BF16)] * 2,
        in_specs=[pl.BlockSpec(memory_space=pl.ANY)] * 2,
        out_specs=[pl.BlockSpec(memory_space=pl.ANY)] * 2,
        scratch_shapes=[pltpu.SemaphoreType.DMA((8,))],
        compiler_params=pltpu.CompilerParams(vmem_limit_bytes=1024 * 1024),
    )(*outs)


def solution(mesh):
    return jax.shard_map(
        per_device,
        mesh=mesh,
        in_specs=(P("past", "second"), P(None, "past"), P(), P(None, "second"), P(None, "second")),
        out_specs=(P(None, "second"), P(None, "second")),
        check_vma=False,
    )
```

time: 50.7 us -> 47.3 us (0.933)
  local copies, waits for them, and re-layouts: 2.64 us -> 0 us
  Pallas kernels: 47.3 us -> 46.6 us
    pallas_call x1, Pallas kernels: 47.3 us -> 44.5 us  [per_device(): pl.pallas_call(functools.partial(kernel, n_z, rows * columns * n_z), out_...]
    unnamed x2 -> x0, local copies, waits for them, and re-layouts: 2.64 us -> none
    pallas_call x0 -> x1, Pallas kernels: none -> 2.07 us  [per_device(): pl.pallas_call(write_out, out_shape=[jax.ShapeDtypeStruct((2 * rows, colu...]
where the time goes in v3:
time: 47.3 us; the launch traced here: 47.2 us
  Pallas kernels  46.6 us (99%)
  between operations  0.64 us (1%)
    pallas_call x1, Pallas kernels, per_device(): pl.pallas_call(functools.partial(kernel, n_z, rows * columns * n_z), out_...  44.5 us
    pallas_call x1, Pallas kernels, per_device(): pl.pallas_call(write_out, out_shape=[jax.ShapeDtypeStruct((2 * rows, colu...  2.07 us

profile of v3, /device:TPU:1, one launch (start us, length us, event | category | flops | bytes accessed | tf_op | source)
XLA Modules:
  0.0 47.2 jit_solution(6478771417947430790)
XLA Ops:
  0.6 44.5 %shard_map.68 = (bf16[1024,1024]{1,0:T(8,128)(2,1)S(1)}, bf16[1024,1024]{1,0:T(8,128)(2,1)S(1)}) custom-call(bf16[2048,1024]{1,0:T(8,128)(2,1)} %g_hbm.1, bf16[1024,2048]{1,0:T(8,128)(2,1)} %sig_hbm.1, bf16[2,512,1024]{2,1,0:T(8,128)(2,1)} %vol_hbm.1, bf16[512,1024]{1,0:T(8,128)(2,1)} %edge_hbm.1, f32[32,1024]{1,0:T(8,128)} %coup_hbm.1), custom_call_target="tpu_custom_call" | custom-call | tf_op jit(solution)/shard_map/pallas_call | solution.py:336
  45.1 2.1 %shard_map.69 = (bf16[1024,1024]{1,0:T(8,128)(2,1)}, bf16[1024,1024]{1,0:T(8,128)(2,1)}) custom-call(bf16[1024,1024]{1,0:T(8,128)(2,1)S(1)} %get-tuple-element.4.g_in, bf16[1024,1024]{1,0:T(8,128)(2,1)S(1)} %get-tuple-element.5.s_in), custom_call_target="tpu_custom_call" | custom-call | tf_op jit(solution)/shard_map/pallas_call | solution.py:367

commit v4 on v3

--- a/solution.py
+++ b/solution.py
@@ -13,6 +13,7 @@
 BF16 = jnp.bfloat16
 RING = 4
 CHUNKS = 4
+ORDER = ((0, 2), (1, 2), (0, 3), (1, 3), (0, 1), (1, 1))
 
 
 def dot(a, b):
@@ -37,33 +38,12 @@
     x = lax.rem(past // 2, RING)
     y = past // (2 * RING)
     partner = (past + 1 - 2 * core, z)
-    def bits(p):
-        return lax.rem((p + 1) // 2, 2), p // 2
-
-    xi, xj = bits(x)
-    yi, yj = bits(y)
-
-    def flip(bit, yes):
-        return 1 - bit if yes else bit
-
-    def position(i, j):
-        return i + j * (3 - 2 * i)
-
-    def face_of(f, d):
-        dx, dy = d % 2, d // 2
-        if f == 0:
-            bx, by = flip(xi, dx), flip(yi, dy)
-            px, py = position(bx, xj), position(by, yj)
-        else:
-            bx, by = flip(xj, dx), flip(yj, dy)
-            px, py = position(xi, bx), position(yi, by)
-        return bx + 2 * by, ((py * RING + px) * 2 + core, z)
-
-    faces = [[face_of(f, d) for d in range(RING)] for f in range(2)]
-    s_of = [[faces[f][d][0] for d in range(RING)] for f in (0, 1)]
-    t_of = [s_of[1], s_of[0]]
-    s_peer = [[faces[f][d][1] for d in range(RING)] for f in (0, 1)]
-    t_peer = [s_peer[1], s_peer[0]]
+    x_of = [lax.rem(x + d, RING) for d in range(RING)]
+    y_of = [lax.rem(y + d, RING) for d in range(RING)]
+    x_peer = [((y * RING + x_of[d]) * 2 + core, z) for d in range(RING)]
+    y_peer = [((y_of[d] * RING + x) * 2 + core, z) for d in range(RING)]
+    s_of, t_of = [x_of, y_of], [y_of, x_of]
+    s_peer, t_peer = [x_peer, y_peer], [y_peer, x_peer]
     z_of = [lax.rem(z + d, n_z) for d in range(n_z)]
     z_peer = [(past, z_of[d]) for d in range(n_z)]
 
@@ -82,13 +62,12 @@
     ld["p0"] = load(sig_hbm.at[sig_rows(0, 1 - core)], sig.at[sig_rows(0, 1 - core)])
     first = [load(g_hbm.at[:, i * tile : (i + 1) * tile], g.at[0, :, i * tile : (i + 1) * tile]) for i in range(width // tile)]
 
-    def load_more():
-        ld["o0"] = load(sig_hbm.at[sig_rows(0, core)], sig.at[sig_rows(0, core)])
-        ld["g1"] = load(g_hbm.at[:, width : 2 * width], g.at[1])
+    ld["g1"] = load(g_hbm.at[:, width : 2 * width], g.at[1])
+    ld["o0"] = load(sig_hbm.at[sig_rows(0, core)], sig.at[sig_rows(0, core)])
+    ld["p1"] = load(sig_hbm.at[sig_rows(1, 1 - core)], sig.at[sig_rows(1, 1 - core)])
+    ld["o1"] = load(sig_hbm.at[sig_rows(1, core)], sig.at[sig_rows(1, core)])
 
     def load_rest():
-        ld["p1"] = load(sig_hbm.at[sig_rows(1, 1 - core)], sig.at[sig_rows(1, 1 - core)])
-        ld["o1"] = load(sig_hbm.at[sig_rows(1, core)], sig.at[sig_rows(1, core)])
         ld["edge"] = load(edge_hbm, edge)
         ld["vol"] = load(vol_hbm, vol)
         ld["coup"] = load(coup_hbm, coup)
@@ -127,8 +106,6 @@
         b, j = k // 2, k % 2
         if j == 0:
             ld[f"p{b}"].wait()
-        if k == 0:
-            load_more()
         if k == 1:
             ld["g1"].wait()
         for i in range(width // tile):
@@ -136,8 +113,9 @@
                 first[i].wait()
             cols = pl.ds(i * tile, tile)
             psend[k, :, cols] = dot(sig[sig_rows(b, 1 - core)], g[j, :, cols])
+        if k == 2:
+            load_rest()
         if k == 0:
-            load_rest()
             pl.semaphore_wait(barrier, len(friends))
         put(("chip", k), psend.at[k], precv.at[k], partner)
 
@@ -155,48 +133,49 @@
     def chip_sum(k):
         arrived(("chip", k), precv.at[k])
         a_buf[k] = (own[k] + precv[k]).astype(BF16)
-        for d in (3, 1, 2):
-            for h in range(2):
-                put(("a", k, h, d), a_buf.at[k, pl.ds(row(h, d), sub)], ra.at[k, h, d - 1], s_peer[h][d])
+        for h, d in ORDER:
+            put(("a", k, h, d), a_buf.at[k, pl.ds(row(h, d), sub)], ra.at[k, h, d - 1], s_peer[h][d])
 
     def ring_sum(k):
         for h in range(2):
             mine = pl.ds(row(h, 0), sub)
             t = t_of[h]
             total = own[k, mine] + precv[k, mine]
-            for d in (2, 1, 3):
+            for d in (1, 3, 2):
                 arrived(("a", k, h, d), ra.at[k, h, d - 1])
                 total = total + ra[k, h, d - 1].astype(F32)
             b_buf[k, h, t[0]] = total.astype(BF16)
-            for d in (3, 1, 2):
-                ref = b_buf.at[k, h, t[0]]
-                put(("b", k, h, d), ref, ref, t_peer[h][d])
+        for h, d in ORDER:
+            ref = b_buf.at[k, h, t_of[h][0]]
+            put(("b", k, h, d), ref, ref, t_peer[h][d])
 
     def mem_at(k, part, h, d):
         return mem.at[k, pl.ds(pl.multiple_of(part * half + row(h, d), sub), sub)]
 
     def plane_sum(k):
         for h in range(2):
-            for d in (2, 1, 3):
-                arrived(("b", k, h, d), b_buf.at[k, h, t_of[h][d]])
+            for d in (1, 3, 2):
+                arrived(("b", k, h, d), b_buf.at[k, h, t_of[h][RING - d]])
             total = b_buf[k, h, 0].astype(F32)
             for i in range(1, RING):
                 total = total + b_buf[k, h, i].astype(F32)
             mem[k, pl.ds(pl.multiple_of(core * half + row(h, 0), sub), sub)] = total.astype(BF16)
+        for h, d in ORDER:
             ref = mem_at(k, core, h, 0)
-            for d in (3, 1, 2):
-                put(("c", k, h, d), ref, ref, s_peer[h][d])
+            put(("c", k, h, d), ref, ref, s_peer[h][d])
+
+    def gather(k):
+        for h in range(2):
+            ref = mem_at(k, core, h, 0)
             put(("f", k, h, 0), ref, ref, partner)
-
-    def gather(k):
-        for d in (2, 1, 3):
+        for d in (1, 3, 2):
             for h in range(2):
-                ref = mem_at(k, core, h, d)
+                ref = mem_at(k, core, h, RING - d)
                 arrived(("c", k, h, d), ref)
-                put(("f", k, h, d), ref, ref, partner)
+                put(("f", k, h, RING - d), ref, ref, partner)
 
     def gathered(k):
-        for d in (0, 2, 1, 3):
+        for d in (0, 3, 1, 2):
             for h in range(2):
                 arrived(("f", k, h, d), mem_at(k, 1 - core, h, d))
 
@@ -215,11 +194,6 @@
         cube = (gnew * gnew * gnew).reshape(rows // N, N, tile) * coup[:, cols][None]
         return cube.reshape(rows, tile)
 
-    def finish(cols, gnew):
-        cube = cube_of(cols, gnew)
-        cubic[:, cols] = cube
-        return fold(cube)
-
     def share(b, total):
         stat[b, z] = total
         for d in range(1, n_z):
@@ -246,11 +220,8 @@
         for i in range(width // tile):
             cols = columns_of(k, i)
             gnew = s_buf[0, :, cols] + dot(vol[0, :, 0:rows], mem[k, :, pl.ds(i * tile, tile)])
-            cube = cube_of(cols, gnew)
-            cubic0[:, cols] = cube
-            cube16[:, cols] = cube.astype(BF16)
-            g_out[0:rows, cols] = gnew.astype(BF16)
-            part = fold(cube)
+            cubic0[:, cols] = gnew
+            part = fold(cube_of(cols, gnew))
             total = part if total is None else total + part
         return total
 
@@ -259,22 +230,19 @@
         for i in range(width // tile):
             s_buf[1, :, columns_of(k, i)] = dot(vol[1, :, 0:rows], mem[k, :, pl.ds(i * tile, tile)])
 
-    product_send(0)
-    product_own(0)
-    for k in range(1, CHUNKS):
-        product_send(k)
-        chip_sum(k - 1)
-        product_own(k)
+    for b in range(2):
+        product_send(2 * b)
+        product_send(2 * b + 1)
+        for k in (2 * b, 2 * b + 1):
+            product_own(k)
+            chip_sum(k)
+    for i in range(4):
+        start_value(i)
     ring_sum(0)
-    chip_sum(3)
-    start_value(0)
     ring_sum(1)
-    start_value(1)
     ring_sum(2)
-    start_value(2)
     plane_sum(0)
     ring_sum(3)
-    start_value(3)
     plane_sum(1)
     plane_sum(2)
     gather(0)
@@ -287,6 +255,13 @@
     gather(3)
     for i in range(2 * width // tile):
         cols = pl.ds(i * tile, tile)
+        gnew = cubic0[:, cols]
+        g_out[0:rows, cols] = gnew.astype(BF16)
+        cube = cube_of(cols, gnew)
+        cubic0[:, cols] = cube
+        cube16[:, cols] = cube.astype(BF16)
+    for i in range(2 * width // tile):
+        cols = pl.ds(i * tile, tile)
         s_buf[0, :, cols] = dot(vol[1, :, rows : 2 * rows], cube16[:, cols])
     second_memory(2)
     second_memory(3)
@@ -296,12 +271,14 @@
         cols = pl.ds(i * tile, tile)
         gnew = s_buf[1, :, cols] + s_buf[0, :, cols] * inv0
         s_buf[1, :, cols] = gnew
-        part = finish(cols, gnew)
+        part = fold(cube_of(cols, gnew))
         total = part if total is None else total + part
     share(1, total)
     for i in range(2 * width // tile):
         cols = pl.ds(i * tile, tile)
-        g_out[rows : 2 * rows, cols] = s_buf[1, :, cols].astype(BF16)
+        gnew = s_buf[1, :, cols]
+        g_out[rows : 2 * rows, cols] = gnew.astype(BF16)
+        cubic[:, cols] = cube_of(cols, gnew)
         s_out[0:rows, cols] = (cubic0[:, cols] * inv0).astype(BF16)
     inv1 = 1.0 / scale_of(1)
     for i in range(2 * width // tile):

time: 47.3 us -> 46.3 us (0.979)
  Pallas kernels: 46.6 us -> 45.5 us
    pallas_call x1, Pallas kernels: 44.5 us -> 43.5 us  [per_device(): pl.pallas_call(functools.partial(kernel, n_z, rows * columns * n_z), out_...]
where the time goes in v4:
time: 46.3 us; the launch traced here: 46.2 us
  Pallas kernels  45.5 us (98%)
  between operations  0.64 us (1%)
    pallas_call x1, Pallas kernels, per_device(): pl.pallas_call(functools.partial(kernel, n_z, rows * columns * n_z), out_...  43.5 us
    pallas_call x1, Pallas kernels, per_device(): pl.pallas_call(write_out, out_shape=[jax.ShapeDtypeStruct((2 * rows, colu...  2.07 us

profile of v4, /device:TPU:1, one launch (start us, length us, event | category | flops | bytes accessed | tf_op | source)
XLA Modules:
  0.0 46.2 jit_solution(18425212762590196168)
XLA Ops:
  0.6 43.5 %shard_map.68 = (bf16[1024,1024]{1,0:T(8,128)(2,1)S(1)}, bf16[1024,1024]{1,0:T(8,128)(2,1)S(1)}) custom-call(bf16[2048,1024]{1,0:T(8,128)(2,1)} %g_hbm.1, bf16[1024,2048]{1,0:T(8,128)(2,1)} %sig_hbm.1, bf16[2,512,1024]{2,1,0:T(8,128)(2,1)} %vol_hbm.1, bf16[512,1024]{1,0:T(8,128)(2,1)} %edge_hbm.1, f32[32,1024]{1,0:T(8,128)} %coup_hbm.1), custom_call_target="tpu_custom_call" | custom-call | tf_op jit(solution)/shard_map/pallas_call | solution.py:313
  44.1 2.1 %shard_map.69 = (bf16[1024,1024]{1,0:T(8,128)(2,1)}, bf16[1024,1024]{1,0:T(8,128)(2,1)}) custom-call(bf16[1024,1024]{1,0:T(8,128)(2,1)S(1)} %get-tuple-element.4.g_in, bf16[1024,1024]{1,0:T(8,128)(2,1)S(1)} %get-tuple-element.5.s_in), custom_call_target="tpu_custom_call" | custom-call | tf_op jit(solution)/shard_map/pallas_call | solution.py:344
